TPU v7x, 128 devices: a whole 4x4x4 slice. The times are simulated.
128 devices in a mesh: tensor: 8 (over y_hi, x), context: 16 (over z, y_lo, core).
Axes of the slice: x: 4, y: 4 (y_hi: 2, y_lo: 2; y = y_hi * 2 + y_lo), z: 4, core: 2. Of those that a mesh axis runs over, the one named last changes fastest.
Arguments:
- tokens: bfloat16 [16, 1024, 4096], P('context', 'tensor'), may hold values from -6 to 6
- norm_gain: float32 [4096], replicated, may hold values from 0.25 to 1.75
- q_weight: bfloat16 [4096, 2048], P(None, 'tensor')
- k_weight: bfloat16 [4096, 1024], P(None, 'tensor')
- v_weight: bfloat16 [4096, 1024], P(None, 'tensor'), may hold values from -0.75 to 0.75
- o_weight: bfloat16 [2048, 4096], P('tensor'), may hold values from -0.125 to 0.125
- doc_lengths: int32 [16], replicated, may hold values from 1 to 4096, 16384 in all
- span_order: int32 [32], replicated, may hold values from 0 to 31, each once
Outputs:
- layer_out: bfloat16 [16, 1024, 4096], P('context', 'tensor')
Inputs may be any that keep to these rules, and one draw needn't show every extreme that they name: `doc_lengths`: documents fill the sequence in order; the longest has exactly 4096 tokens. `span_order`: each value appears once.
All inputs are finite; a program needn't handle non-finite values.
Results may differ from a plain program's by a relative error of at most 0.019.
Values may be sent and summed in bfloat16 or wider, within the bound.
A program may use at most 320 MiB of HBM per device.

v0:
```python
import math
import jax
import jax.numpy as jnp
from jax import lax
from jax.sharding import PartitionSpec as P

HEAD_DIM = 128
rope_theta = 500000.0
epsilon = 1e-05
masked_score = -1e30


def positions(rows, span_order, span_rows):
    slot_ids = jnp.arange(span_order.shape[0], dtype=jnp.int32)
    matches = (rows // span_rows)[:, None] == slot_ids[None, :]
    picked = jnp.sum(jnp.where(matches, span_order[None, :], 0), axis=1)
    return picked * span_rows + rows % span_rows


def documents(places, doc_lengths):
    doc_ends = jnp.cumsum(doc_lengths)
    return jnp.sum((doc_ends[None, :] <= places[:, None]).astype(jnp.int32), axis=1)


def rotary(values, places):
    head_dim = values.shape[-1]
    half_dim = head_dim // 2
    frequency = rope_theta ** (-(2.0 / head_dim) * jnp.arange(half_dim, dtype=jnp.float32))
    angles = places.astype(jnp.float32)[:, None] * frequency[None, :]
    cosine = jnp.cos(angles)[:, None, :]
    sine_part = jnp.sin(angles)[:, None, :]
    first_half = values[..., :half_dim]
    second = values[..., half_dim:]
    return jnp.concatenate(
        [first_half * cosine - second * sine_part, second * cosine + first_half * sine_part],
        axis=-1,
    )


def per_device(tokens, norm_gain, q_weight, k_weight, v_weight, o_weight, doc_lengths, span_order):
    local_rows = tokens.shape[1]
    tok_dev = local_rows * lax.axis_size("tensor")
    model_width = tokens.shape[2]
    head_dim = HEAD_DIM
    q_cols = q_weight.shape[1]
    kv_cols = k_weight.shape[1]
    q_heads = q_cols // head_dim
    kv_local = kv_cols // head_dim
    group_size = q_heads // kv_local
    span_rows = tok_dev // 2
    base_row = lax.axis_index("context") * tok_dev
    score_scale = 1.0 / math.sqrt(head_dim)
    rows_float = tokens.astype(jnp.float32)
    normed = (
        rows_float
        * lax.rsqrt(jnp.mean(rows_float * rows_float, axis=-1, keepdims=True) + epsilon)
        * norm_gain
    ).astype(jnp.bfloat16)
    portion = lax.all_gather(normed, "tensor", axis=1, tiled=True)
    row_count = portion.shape[1]
    flat_rows = portion.reshape(row_count, model_width)
    places = positions(base_row + jnp.arange(row_count, dtype=jnp.int32), span_order, span_rows)
    query_rows = jnp.dot(flat_rows, q_weight, preferred_element_type=jnp.float32).reshape(
        row_count, q_heads, head_dim
    )
    key_rows = jnp.dot(flat_rows, k_weight, preferred_element_type=jnp.float32).reshape(
        row_count, kv_local, head_dim
    )
    value_rows = jnp.dot(flat_rows, v_weight, preferred_element_type=jnp.float32).astype(
        jnp.bfloat16
    )
    query_rows = rotary(query_rows, places).reshape(row_count, q_cols).astype(jnp.bfloat16)
    key_rows = rotary(key_rows, places).reshape(row_count, kv_cols).astype(jnp.bfloat16)
    projected = jnp.concatenate([query_rows, key_rows, value_rows], axis=1)[None][0]
    query_places = positions(base_row + jnp.arange(tok_dev, dtype=jnp.int32), span_order, span_rows)
    query_docs = documents(query_places, doc_lengths)
    queries = projected[:, :q_cols].reshape(tok_dev, kv_local, group_size, head_dim)
    kv_pair = jnp.stack([projected[:, q_cols : q_cols + kv_cols], projected[:, q_cols + kv_cols :]])

    def attend(running, portion, offset):
        row_count = portion.shape[1]
        key_places = positions(
            offset + jnp.arange(row_count, dtype=jnp.int32), span_order, span_rows
        )
        key_docs = documents(key_places, doc_lengths)
        visible = (key_places[None, :] <= query_places[:, None]) & (
            key_docs[None, :] == query_docs[:, None]
        )
        running_max, row_sum, weighted = running
        key_rows = portion[0].reshape(row_count, kv_local, head_dim)
        value_rows = portion[1].reshape(row_count, kv_local, head_dim)
        scores = (
            jnp.einsum("qkgd,skd->kgqs", queries, key_rows, preferred_element_type=jnp.float32)
            * score_scale
        )
        limited = jnp.where(visible, scores, masked_score)
        new_max = jnp.maximum(running_max, jnp.max(limited, axis=-1))
        factor = jnp.exp(running_max - new_max)
        weights = jnp.where(visible, jnp.exp(scores - new_max[..., None]), 0.0)
        row_sum = row_sum * factor + jnp.sum(weights, axis=-1)
        weighted = weighted * factor.transpose(2, 0, 1)[..., None] + jnp.einsum(
            "kgqs,skd->qkgd",
            weights.astype(jnp.bfloat16),
            value_rows,
            preferred_element_type=jnp.float32,
        )
        return (new_max, row_sum, weighted)

    initial = (
        jnp.full((kv_local, group_size, tok_dev), masked_score, jnp.float32),
        jnp.zeros((kv_local, group_size, tok_dev), jnp.float32),
        jnp.zeros((tok_dev, kv_local, group_size, head_dim), jnp.float32),
    )
    gathered = lax.all_gather(kv_pair, "context", axis=1, tiled=True)

    def visit_block(block_index, carried):
        offset = block_index * tok_dev
        portion = lax.dynamic_slice_in_dim(gathered, offset, tok_dev, 1)
        return attend(carried, portion, offset)

    running_max, row_sum, weighted = lax.fori_loop(
        0, lax.axis_size("context"), visit_block, initial
    )
    attended = (
        (weighted / row_sum.transpose(2, 0, 1)[..., None])
        .reshape(tok_dev, q_cols)
        .astype(jnp.bfloat16)
    )
    mixed_rows = lax.psum_scatter(
        jnp.dot(attended, o_weight, preferred_element_type=jnp.float32).astype(jnp.bfloat16),
        "tensor",
        scatter_dimension=0,
        tiled=True,
    )
    return mixed_rows.reshape(tokens.shape)


def solution(mesh):
    in_specs = (
        P("context", "tensor", None),
        P(),
        P(None, "tensor"),
        P(None, "tensor"),
        P(None, "tensor"),
        P("tensor", None),
        P(),
        P(),
    )
    out_specs = P("context", "tensor", None)
    return jax.shard_map(
        per_device, mesh=mesh, in_specs=in_specs, out_specs=out_specs, check_vma=False
    )
```

profile of v0, /device:TPU:1, one launch (start us, length us, event | category | flops | bytes accessed | tf_op | source)
XLA Modules:
  0.0 585.3 jit_solution(13166002887668406212)
XLA Ops:
  6.5 1.7 fusion.34
  8.2 2.5 fusion.36
  11.7 110.9 %all-gather.3.cloned.1.call-done = bf16[1,1024,4096]{2,1,0:T(8,128)(2,1)} async-done(((bf16[1,128,4096]{2,1,0:T(8,128)(2,1)}), bf16[1,1024,4096]{2,1,0:T(8,128)(2,1)}) %all-gather.3.cloned.1.call-update) | async-done | bytes 8388624 | tf_op jit(solution)/shard_map/all_gather | solution.py:59
  122.6 6.7 %fusion.37 = f32[1024,1,128]{0,2,1:T(8,128)S(1)} fusion(bf16[4096,128]{1,0:T(8,128)(2,1)} %param.13, bf16[1,1024,4096]{2,1,0:T(8,128)(2,1)} %all-gather.3.cloned.1.call-done), kind=kOutput, calls=%fused_computation.56 | convolution fusion | flops 1073741824 | bytes 9961472 | tf_op jit(solution)/shard_map/dot_general | solution.py:66
  130.5 2.9 fusion.43
  134.5 4.1 copy.24
  139.9 6.7 %fusion.28 = f32[1024,2,128]{0,2,1:T(8,128)S(1)} fusion(bf16[2,128,4096]{2,1,0:T(8,128)(2,1)} %bitcast.129, bf16[1,1024,4096]{2,1,0:T(8,128)(2,1)} %all-gather.3.cloned.1.call-done), kind=kOutput, calls=%fused_computation.44 | convolution fusion | flops 2147483648 | bytes 11534336 | tf_op jit(solution)/shard_map/dot_general | solution.py:63
  147.8 37.5 %all-gather.5.cloned.1.call-done = bf16[2,16384,128]{1,2,0:T(8,128)(2,1)} async-done(((bf16[2,1024,128]{1,2,0:T(8,128)(2,1)}), bf16[2,16384,128]{1,2,0:T(8,128)(2,1)}) %all-gather.5.cloned.1.call-update) | async-done | bytes 8388624 | tf_op jit(solution)/shard_map/all_gather | solution.py:114
  185.3 270.9 %while.20 = (s32[]{:T(128)}, f32[1,2,1024]{2,1,0:T(2,128)S(1)}, f32[1,2,1024]{2,1,0:T(2,128)S(1)}, f32[1024,1,2,128]{0,3,2,1:T(8,128)}, s32[32]{0:T(128)S(1)}, /...) while((s32[]{:T(128)}, f32[1,2,1024]{2,1,0:T(2,128)S(1)}, ...), condition=%wide.region_9.10_spmd.clone, body=%wide.region_4.9_spmd.clone.sunk | while | flops 1100931072 | bytes 66236864 | solution.py:121
  186.7 6.3 %fusion.77 = (f32[2,1024]{1,0:T(2,128)S(1)}, f32[1024,1024,2]{1,0,2:T(8,128)}) fusion(pred[1024,1024]{0,1:T(8,128)(4,1)S(1)} %compare_and_fusion.2, bf16[1024,1,2,128]{3,0,2,1:T(8,128)(2,1)} %get-tuple-element.448, bf16[2,16384,128]{1,2,0:T(8,128)(2,1)} %get-tuple-element.447, s32[]{:T(128)S(6)} %select_n.164), kind=kOutput, calls=%fused_computation.2.clone.1 | convolution fusion | flops 543160320 | bytes 10231812 | tf_op jit(solution)/shard_map/while/body/eval_jaxpr/qkgd,skd->kgqs/dot_general | solution.py:93
  193.0 7.0 %fusion.80 = f32[1024,1,2,128]{0,3,2,1:T(8,128)} fusion(f32[1024,1024,2]{1,0,2:T(8,128)} %get-tuple-element.407, f32[2,1024]{1,0:T(2,128)S(1)} %bitcast.126, pred[1024,1024]{0,1:T(8,128)(4,1)S(1)} %compare_and_fusion.2, f32[1024,1,2,128]{0,3,2,1:T(8,128)} %get-tuple-element.427, f32[1024,2]{0,1:T(2,128)S(1)} %get-tuple-element.408, ...), kind=kOutput, calls=%fused_computation.12.clone.1 | convolution fusion | flops 546045952 | bytes 11812873 | tf_op jit(solution)/shard_map/while/body/eval_jaxpr/kgqs,skd->qkgd/dot_general | solution.py:101
  200.0 2.0 fusion.79
  202.2 1.2 compare_and_fusion.2
  203.5 6.3 %fusion.77 = (f32[2,1024]{1,0:T(2,128)S(1)}, f32[1024,1024,2]{1,0,2:T(8,128)}) fusion(pred[1024,1024]{0,1:T(8,128)(4,1)S(1)} %compare_and_fusion.2, bf16[1024,1,2,128]{3,0,2,1:T(8,128)(2,1)} %get-tuple-element.448, bf16[2,16384,128]{1,2,0:T(8,128)(2,1)} %get-tuple-element.447, s32[]{:T(128)S(6)} %select_n.164), kind=kOutput, calls=%fused_computation.2.clone.1 | convolution fusion | flops 543160320 | bytes 10231812 | tf_op jit(solution)/shard_map/while/body/eval_jaxpr/qkgd,skd->kgqs/dot_general | solution.py:93
  209.8 7.2 %fusion.80 = f32[1024,1,2,128]{0,3,2,1:T(8,128)} fusion(f32[1024,1024,2]{1,0,2:T(8,128)} %get-tuple-element.407, f32[2,1024]{1,0:T(2,128)S(1)} %bitcast.126, pred[1024,1024]{0,1:T(8,128)(4,1)S(1)} %compare_and_fusion.2, f32[1024,1,2,128]{0,3,2,1:T(8,128)} %get-tuple-element.427, f32[1024,2]{0,1:T(2,128)S(1)} %get-tuple-element.408, ...), kind=kOutput, calls=%fused_computation.12.clone.1 | convolution fusion | flops 546045952 | bytes 11812873 | tf_op jit(solution)/shard_map/while/body/eval_jaxpr/kgqs,skd->qkgd/dot_general | solution.py:101
  217.0 2.0 fusion.79
  220.4 6.3 %fusion.77 = (f32[2,1024]{1,0:T(2,128)S(1)}, f32[1024,1024,2]{1,0,2:T(8,128)}) fusion(pred[1024,1024]{0,1:T(8,128)(4,1)S(1)} %compare_and_fusion.2, bf16[1024,1,2,128]{3,0,2,1:T(8,128)(2,1)} %get-tuple-element.448, bf16[2,16384,128]{1,2,0:T(8,128)(2,1)} %get-tuple-element.447, s32[]{:T(128)S(6)} %select_n.164), kind=kOutput, calls=%fused_computation.2.clone.1 | convolution fusion | flops 543160320 | bytes 10231812 | tf_op jit(solution)/shard_map/while/body/eval_jaxpr/qkgd,skd->kgqs/dot_general | solution.py:93
  226.7 7.2 %fusion.80 = f32[1024,1,2,128]{0,3,2,1:T(8,128)} fusion(f32[1024,1024,2]{1,0,2:T(8,128)} %get-tuple-element.407, f32[2,1024]{1,0:T(2,128)S(1)} %bitcast.126, pred[1024,1024]{0,1:T(8,128)(4,1)S(1)} %compare_and_fusion.2, f32[1024,1,2,128]{0,3,2,1:T(8,128)} %get-tuple-element.427, f32[1024,2]{0,1:T(2,128)S(1)} %get-tuple-element.408, ...), kind=kOutput, calls=%fused_computation.12.clone.1 | convolution fusion | flops 546045952 | bytes 11812873 | tf_op jit(solution)/shard_map/while/body/eval_jaxpr/kgqs,skd->qkgd/dot_general | solution.py:101
  233.9 2.0 fusion.79
  237.4 6.3 %fusion.77 = (f32[2,1024]{1,0:T(2,128)S(1)}, f32[1024,1024,2]{1,0,2:T(8,128)}) fusion(pred[1024,1024]{0,1:T(8,128)(4,1)S(1)} %compare_and_fusion.2, bf16[1024,1,2,128]{3,0,2,1:T(8,128)(2,1)} %get-tuple-element.448, bf16[2,16384,128]{1,2,0:T(8,128)(2,1)} %get-tuple-element.447, s32[]{:T(128)S(6)} %select_n.164), kind=kOutput, calls=%fused_computation.2.clone.1 | convolution fusion | flops 543160320 | bytes 10231812 | tf_op jit(solution)/shard_map/while/body/eval_jaxpr/qkgd,skd->kgqs/dot_general | solution.py:93
  243.7 7.2 %fusion.80 = f32[1024,1,2,128]{0,3,2,1:T(8,128)} fusion(f32[1024,1024,2]{1,0,2:T(8,128)} %get-tuple-element.407, f32[2,1024]{1,0:T(2,128)S(1)} %bitcast.126, pred[1024,1024]{0,1:T(8,128)(4,1)S(1)} %compare_and_fusion.2, f32[1024,1,2,128]{0,3,2,1:T(8,128)} %get-tuple-element.427, f32[1024,2]{0,1:T(2,128)S(1)} %get-tuple-element.408, ...), kind=kOutput, calls=%fused_computation.12.clone.1 | convolution fusion | flops 546045952 | bytes 11812873 | tf_op jit(solution)/shard_map/while/body/eval_jaxpr/kgqs,skd->qkgd/dot_general | solution.py:101
  250.9 2.0 fusion.79
  253.1 1.2 compare_and_fusion.2
  254.3 6.3 %fusion.77 = (f32[2,1024]{1,0:T(2,128)S(1)}, f32[1024,1024,2]{1,0,2:T(8,128)}) fusion(pred[1024,1024]{0,1:T(8,128)(4,1)S(1)} %compare_and_fusion.2, bf16[1024,1,2,128]{3,0,2,1:T(8,128)(2,1)} %get-tuple-element.448, bf16[2,16384,128]{1,2,0:T(8,128)(2,1)} %get-tuple-element.447, s32[]{:T(128)S(6)} %select_n.164), kind=kOutput, calls=%fused_computation.2.clone.1 | convolution fusion | flops 543160320 | bytes 10231812 | tf_op jit(solution)/shard_map/while/body/eval_jaxpr/qkgd,skd->kgqs/dot_general | solution.py:93
  260.6 7.2 %fusion.80 = f32[1024,1,2,128]{0,3,2,1:T(8,128)} fusion(f32[1024,1024,2]{1,0,2:T(8,128)} %get-tuple-element.407, f32[2,1024]{1,0:T(2,128)S(1)} %bitcast.126, pred[1024,1024]{0,1:T(8,128)(4,1)S(1)} %compare_and_fusion.2, f32[1024,1,2,128]{0,3,2,1:T(8,128)} %get-tuple-element.427, f32[1024,2]{0,1:T(2,128)S(1)} %get-tuple-element.408, ...), kind=kOutput, calls=%fused_computation.12.clone.1 | convolution fusion | flops 546045952 | bytes 11812873 | tf_op jit(solution)/shard_map/while/body/eval_jaxpr/kgqs,skd->qkgd/dot_general | solution.py:101
  267.8 2.0 fusion.79
  271.2 6.3 %fusion.77 = (f32[2,1024]{1,0:T(2,128)S(1)}, f32[1024,1024,2]{1,0,2:T(8,128)}) fusion(pred[1024,1024]{0,1:T(8,128)(4,1)S(1)} %compare_and_fusion.2, bf16[1024,1,2,128]{3,0,2,1:T(8,128)(2,1)} %get-tuple-element.448, bf16[2,16384,128]{1,2,0:T(8,128)(2,1)} %get-tuple-element.447, s32[]{:T(128)S(6)} %select_n.164), kind=kOutput, calls=%fused_computation.2.clone.1 | convolution fusion | flops 543160320 | bytes 10231812 | tf_op jit(solution)/shard_map/while/body/eval_jaxpr/qkgd,skd->kgqs/dot_general | solution.py:93
  277.5 7.2 %fusion.80 = f32[1024,1,2,128]{0,3,2,1:T(8,128)} fusion(f32[1024,1024,2]{1,0,2:T(8,128)} %get-tuple-element.407, f32[2,1024]{1,0:T(2,128)S(1)} %bitcast.126, pred[1024,1024]{0,1:T(8,128)(4,1)S(1)} %compare_and_fusion.2, f32[1024,1,2,128]{0,3,2,1:T(8,128)} %get-tuple-element.427, f32[1024,2]{0,1:T(2,128)S(1)} %get-tuple-element.408, ...), kind=kOutput, calls=%fused_computation.12.clone.1 | convolution fusion | flops 546045952 | bytes 11812873 | tf_op jit(solution)/shard_map/while/body/eval_jaxpr/kgqs,skd->qkgd/dot_general | solution.py:101
  284.7 2.0 fusion.79
  287.0 1.2 compare_and_fusion.2
  288.2 6.3 %fusion.77 = (f32[2,1024]{1,0:T(2,128)S(1)}, f32[1024,1024,2]{1,0,2:T(8,128)}) fusion(pred[1024,1024]{0,1:T(8,128)(4,1)S(1)} %compare_and_fusion.2, bf16[1024,1,2,128]{3,0,2,1:T(8,128)(2,1)} %get-tuple-element.448, bf16[2,16384,128]{1,2,0:T(8,128)(2,1)} %get-tuple-element.447, s32[]{:T(128)S(6)} %select_n.164), kind=kOutput, calls=%fused_computation.2.clone.1 | convolution fusion | flops 543160320 | bytes 10231812 | tf_op jit(solution)/shard_map/while/body/eval_jaxpr/qkgd,skd->kgqs/dot_general | solution.py:93
  294.5 7.2 %fusion.80 = f32[1024,1,2,128]{0,3,2,1:T(8,128)} fusion(f32[1024,1024,2]{1,0,2:T(8,128)} %get-tuple-element.407, f32[2,1024]{1,0:T(2,128)S(1)} %bitcast.126, pred[1024,1024]{0,1:T(8,128)(4,1)S(1)} %compare_and_fusion.2, f32[1024,1,2,128]{0,3,2,1:T(8,128)} %get-tuple-element.427, f32[1024,2]{0,1:T(2,128)S(1)} %get-tuple-element.408, ...), kind=kOutput, calls=%fused_computation.12.clone.1 | convolution fusion | flops 546045952 | bytes 11812873 | tf_op jit(solution)/shard_map/while/body/eval_jaxpr/kgqs,skd->qkgd/dot_general | solution.py:101
  301.7 2.0 fusion.79
  305.1 6.3 %fusion.77 = (f32[2,1024]{1,0:T(2,128)S(1)}, f32[1024,1024,2]{1,0,2:T(8,128)}) fusion(pred[1024,1024]{0,1:T(8,128)(4,1)S(1)} %compare_and_fusion.2, bf16[1024,1,2,128]{3,0,2,1:T(8,128)(2,1)} %get-tuple-element.448, bf16[2,16384,128]{1,2,0:T(8,128)(2,1)} %get-tuple-element.447, s32[]{:T(128)S(6)} %select_n.164), kind=kOutput, calls=%fused_computation.2.clone.1 | convolution fusion | flops 543160320 | bytes 10231812 | tf_op jit(solution)/shard_map/while/body/eval_jaxpr/qkgd,skd->kgqs/dot_general | solution.py:93
  311.4 7.2 %fusion.80 = f32[1024,1,2,128]{0,3,2,1:T(8,128)} fusion(f32[1024,1024,2]{1,0,2:T(8,128)} %get-tuple-element.407, f32[2,1024]{1,0:T(2,128)S(1)} %bitcast.126, pred[1024,1024]{0,1:T(8,128)(4,1)S(1)} %compare_and_fusion.2, f32[1024,1,2,128]{0,3,2,1:T(8,128)} %get-tuple-element.427, f32[1024,2]{0,1:T(2,128)S(1)} %get-tuple-element.408, ...), kind=kOutput, calls=%fused_computation.12.clone.1 | convolution fusion | flops 546045952 | bytes 11812873 | tf_op jit(solution)/shard_map/while/body/eval_jaxpr/kgqs,skd->qkgd/dot_general | solution.py:101
  318.6 2.0 fusion.79
  322.1 6.3 %fusion.77 = (f32[2,1024]{1,0:T(2,128)S(1)}, f32[1024,1024,2]{1,0,2:T(8,128)}) fusion(pred[1024,1024]{0,1:T(8,128)(4,1)S(1)} %compare_and_fusion.2, bf16[1024,1,2,128]{3,0,2,1:T(8,128)(2,1)} %get-tuple-element.448, bf16[2,16384,128]{1,2,0:T(8,128)(2,1)} %get-tuple-element.447, s32[]{:T(128)S(6)} %select_n.164), kind=kOutput, calls=%fused_computation.2.clone.1 | convolution fusion | flops 543160320 | bytes 10231812 | tf_op jit(solution)/shard_map/while/body/eval_jaxpr/qkgd,skd->kgqs/dot_general | solution.py:93
  328.4 7.2 %fusion.80 = f32[1024,1,2,128]{0,3,2,1:T(8,128)} fusion(f32[1024,1024,2]{1,0,2:T(8,128)} %get-tuple-element.407, f32[2,1024]{1,0:T(2,128)S(1)} %bitcast.126, pred[1024,1024]{0,1:T(8,128)(4,1)S(1)} %compare_and_fusion.2, f32[1024,1,2,128]{0,3,2,1:T(8,128)} %get-tuple-element.427, f32[1024,2]{0,1:T(2,128)S(1)} %get-tuple-element.408, ...), kind=kOutput, calls=%fused_computation.12.clone.1 | convolution fusion | flops 546045952 | bytes 11812873 | tf_op jit(solution)/shard_map/while/body/eval_jaxpr/kgqs,skd->qkgd/dot_general | solution.py:101
  335.6 2.0 fusion.79
  339.0 6.3 %fusion.77 = (f32[2,1024]{1,0:T(2,128)S(1)}, f32[1024,1024,2]{1,0,2:T(8,128)}) fusion(pred[1024,1024]{0,1:T(8,128)(4,1)S(1)} %compare_and_fusion.2, bf16[1024,1,2,128]{3,0,2,1:T(8,128)(2,1)} %get-tuple-element.448, bf16[2,16384,128]{1,2,0:T(8,128)(2,1)} %get-tuple-element.447, s32[]{:T(128)S(6)} %select_n.164), kind=kOutput, calls=%fused_computation.2.clone.1 | convolution fusion | flops 543160320 | bytes 10231812 | tf_op jit(solution)/shard_map/while/body/eval_jaxpr/qkgd,skd->kgqs/dot_general | solution.py:93
  345.3 7.2 %fusion.80 = f32[1024,1,2,128]{0,3,2,1:T(8,128)} fusion(f32[1024,1024,2]{1,0,2:T(8,128)} %get-tuple-element.407, f32[2,1024]{1,0:T(2,128)S(1)} %bitcast.126, pred[1024,1024]{0,1:T(8,128)(4,1)S(1)} %compare_and_fusion.2, f32[1024,1,2,128]{0,3,2,1:T(8,128)} %get-tuple-element.427, f32[1024,2]{0,1:T(2,128)S(1)} %get-tuple-element.408, ...), kind=kOutput, calls=%fused_computation.12.clone.1 | convolution fusion | flops 546045952 | bytes 11812873 | tf_op jit(solution)/shard_map/while/body/eval_jaxpr/kgqs,skd->qkgd/dot_general | solution.py:101
  352.5 2.0 fusion.79
  356.0 6.3 %fusion.77 = (f32[2,1024]{1,0:T(2,128)S(1)}, f32[1024,1024,2]{1,0,2:T(8,128)}) fusion(pred[1024,1024]{0,1:T(8,128)(4,1)S(1)} %compare_and_fusion.2, bf16[1024,1,2,128]{3,0,2,1:T(8,128)(2,1)} %get-tuple-element.448, bf16[2,16384,128]{1,2,0:T(8,128)(2,1)} %get-tuple-element.447, s32[]{:T(128)S(6)} %select_n.164), kind=kOutput, calls=%fused_computation.2.clone.1 | convolution fusion | flops 543160320 | bytes 10231812 | tf_op jit(solution)/shard_map/while/body/eval_jaxpr/qkgd,skd->kgqs/dot_general | solution.py:93
  362.3 7.2 %fusion.80 = f32[1024,1,2,128]{0,3,2,1:T(8,128)} fusion(f32[1024,1024,2]{1,0,2:T(8,128)} %get-tuple-element.407, f32[2,1024]{1,0:T(2,128)S(1)} %bitcast.126, pred[1024,1024]{0,1:T(8,128)(4,1)S(1)} %compare_and_fusion.2, f32[1024,1,2,128]{0,3,2,1:T(8,128)} %get-tuple-element.427, f32[1024,2]{0,1:T(2,128)S(1)} %get-tuple-element.408, ...), kind=kOutput, calls=%fused_computation.12.clone.1 | convolution fusion | flops 546045952 | bytes 11812873 | tf_op jit(solution)/shard_map/while/body/eval_jaxpr/kgqs,skd->qkgd/dot_general | solution.py:101
  369.5 2.0 fusion.79
  372.9 6.3 %fusion.77 = (f32[2,1024]{1,0:T(2,128)S(1)}, f32[1024,1024,2]{1,0,2:T(8,128)}) fusion(pred[1024,1024]{0,1:T(8,128)(4,1)S(1)} %compare_and_fusion.2, bf16[1024,1,2,128]{3,0,2,1:T(8,128)(2,1)} %get-tuple-element.448, bf16[2,16384,128]{1,2,0:T(8,128)(2,1)} %get-tuple-element.447, s32[]{:T(128)S(6)} %select_n.164), kind=kOutput, calls=%fused_computation.2.clone.1 | convolution fusion | flops 543160320 | bytes 10231812 | tf_op jit(solution)/shard_map/while/body/eval_jaxpr/qkgd,skd->kgqs/dot_general | solution.py:93
  379.2 7.2 %fusion.80 = f32[1024,1,2,128]{0,3,2,1:T(8,128)} fusion(f32[1024,1024,2]{1,0,2:T(8,128)} %get-tuple-element.407, f32[2,1024]{1,0:T(2,128)S(1)} %bitcast.126, pred[1024,1024]{0,1:T(8,128)(4,1)S(1)} %compare_and_fusion.2, f32[1024,1,2,128]{0,3,2,1:T(8,128)} %get-tuple-element.427, f32[1024,2]{0,1:T(2,128)S(1)} %get-tuple-element.408, ...), kind=kOutput, calls=%fused_computation.12.clone.1 | convolution fusion | flops 546045952 | bytes 11812873 | tf_op jit(solution)/shard_map/while/body/eval_jaxpr/kgqs,skd->qkgd/dot_general | solution.py:101
  386.4 2.0 fusion.79
  389.9 6.3 %fusion.77 = (f32[2,1024]{1,0:T(2,128)S(1)}, f32[1024,1024,2]{1,0,2:T(8,128)}) fusion(pred[1024,1024]{0,1:T(8,128)(4,1)S(1)} %compare_and_fusion.2, bf16[1024,1,2,128]{3,0,2,1:T(8,128)(2,1)} %get-tuple-element.448, bf16[2,16384,128]{1,2,0:T(8,128)(2,1)} %get-tuple-element.447, s32[]{:T(128)S(6)} %select_n.164), kind=kOutput, calls=%fused_computation.2.clone.1 | convolution fusion | flops 543160320 | bytes 10231812 | tf_op jit(solution)/shard_map/while/body/eval_jaxpr/qkgd,skd->kgqs/dot_general | solution.py:93
  396.2 7.2 %fusion.80 = f32[1024,1,2,128]{0,3,2,1:T(8,128)} fusion(f32[1024,1024,2]{1,0,2:T(8,128)} %get-tuple-element.407, f32[2,1024]{1,0:T(2,128)S(1)} %bitcast.126, pred[1024,1024]{0,1:T(8,128)(4,1)S(1)} %compare_and_fusion.2, f32[1024,1,2,128]{0,3,2,1:T(8,128)} %get-tuple-element.427, f32[1024,2]{0,1:T(2,128)S(1)} %get-tuple-element.408, ...), kind=kOutput, calls=%fused_computation.12.clone.1 | convolution fusion | flops 546045952 | bytes 11812873 | tf_op jit(solution)/shard_map/while/body/eval_jaxpr/kgqs,skd->qkgd/dot_general | solution.py:101
  403.4 2.0 fusion.79
  405.6 1.2 compare_and_fusion.2
  406.8 6.3 %fusion.77 = (f32[2,1024]{1,0:T(2,128)S(1)}, f32[1024,1024,2]{1,0,2:T(8,128)}) fusion(pred[1024,1024]{0,1:T(8,128)(4,1)S(1)} %compare_and_fusion.2, bf16[1024,1,2,128]{3,0,2,1:T(8,128)(2,1)} %get-tuple-element.448, bf16[2,16384,128]{1,2,0:T(8,128)(2,1)} %get-tuple-element.447, s32[]{:T(128)S(6)} %select_n.164), kind=kOutput, calls=%fused_computation.2.clone.1 | convolution fusion | flops 543160320 | bytes 10231812 | tf_op jit(solution)/shard_map/while/body/eval_jaxpr/qkgd,skd->kgqs/dot_general | solution.py:93
  413.1 7.2 %fusion.80 = f32[1024,1,2,128]{0,3,2,1:T(8,128)} fusion(f32[1024,1024,2]{1,0,2:T(8,128)} %get-tuple-element.407, f32[2,1024]{1,0:T(2,128)S(1)} %bitcast.126, pred[1024,1024]{0,1:T(8,128)(4,1)S(1)} %compare_and_fusion.2, f32[1024,1,2,128]{0,3,2,1:T(8,128)} %get-tuple-element.427, f32[1024,2]{0,1:T(2,128)S(1)} %get-tuple-element.408, ...), kind=kOutput, calls=%fused_computation.12.clone.1 | convolution fusion | flops 546045952 | bytes 11812873 | tf_op jit(solution)/shard_map/while/body/eval_jaxpr/kgqs,skd->qkgd/dot_general | solution.py:101
  420.3 2.0 fusion.79
  423.8 6.3 %fusion.77 = (f32[2,1024]{1,0:T(2,128)S(1)}, f32[1024,1024,2]{1,0,2:T(8,128)}) fusion(pred[1024,1024]{0,1:T(8,128)(4,1)S(1)} %compare_and_fusion.2, bf16[1024,1,2,128]{3,0,2,1:T(8,128)(2,1)} %get-tuple-element.448, bf16[2,16384,128]{1,2,0:T(8,128)(2,1)} %get-tuple-element.447, s32[]{:T(128)S(6)} %select_n.164), kind=kOutput, calls=%fused_computation.2.clone.1 | convolution fusion | flops 543160320 | bytes 10231812 | tf_op jit(solution)/shard_map/while/body/eval_jaxpr/qkgd,skd->kgqs/dot_general | solution.py:93
  430.1 7.2 %fusion.80 = f32[1024,1,2,128]{0,3,2,1:T(8,128)} fusion(f32[1024,1024,2]{1,0,2:T(8,128)} %get-tuple-element.407, f32[2,1024]{1,0:T(2,128)S(1)} %bitcast.126, pred[1024,1024]{0,1:T(8,128)(4,1)S(1)} %compare_and_fusion.2, f32[1024,1,2,128]{0,3,2,1:T(8,128)} %get-tuple-element.427, f32[1024,2]{0,1:T(2,128)S(1)} %get-tuple-element.408, ...), kind=kOutput, calls=%fused_computation.12.clone.1 | convolution fusion | flops 546045952 | bytes 11812873 | tf_op jit(solution)/shard_map/while/body/eval_jaxpr/kgqs,skd->qkgd/dot_general | solution.py:101
  437.3 2.0 fusion.79
  440.7 6.3 %fusion.77 = (f32[2,1024]{1,0:T(2,128)S(1)}, f32[1024,1024,2]{1,0,2:T(8,128)}) fusion(pred[1024,1024]{0,1:T(8,128)(4,1)S(1)} %compare_and_fusion.2, bf16[1024,1,2,128]{3,0,2,1:T(8,128)(2,1)} %get-tuple-element.448, bf16[2,16384,128]{1,2,0:T(8,128)(2,1)} %get-tuple-element.447, s32[]{:T(128)S(6)} %select_n.164), kind=kOutput, calls=%fused_computation.2.clone.1 | convolution fusion | flops 543160320 | bytes 10231812 | tf_op jit(solution)/shard_map/while/body/eval_jaxpr/qkgd,skd->kgqs/dot_general | solution.py:93
  447.0 7.2 %fusion.80 = f32[1024,1,2,128]{0,3,2,1:T(8,128)} fusion(f32[1024,1024,2]{1,0,2:T(8,128)} %get-tuple-element.407, f32[2,1024]{1,0:T(2,128)S(1)} %bitcast.126, pred[1024,1024]{0,1:T(8,128)(4,1)S(1)} %compare_and_fusion.2, f32[1024,1,2,128]{0,3,2,1:T(8,128)} %get-tuple-element.427, f32[1024,2]{0,1:T(2,128)S(1)} %get-tuple-element.408, ...), kind=kOutput, calls=%fused_computation.12.clone.1 | convolution fusion | flops 546045952 | bytes 11812873 | tf_op jit(solution)/shard_map/while/body/eval_jaxpr/kgqs,skd->qkgd/dot_general | solution.py:101
  454.2 2.0 fusion.79
  456.2 1.3 divide_convert_fusion
  457.6 5.6 convolution_convert_fusion
  463.2 115.5 %reduce-scatter.2.cloned.1.call-done = bf16[128,4096]{1,0:T(8,128)(2,1)} async-done(((bf16[1024,4096]{1,0:T(8,128)(2,1)}), bf16[128,4096]{1,0:T(8,128)(2,1)}) %reduce-scatter.2.cloned.1.call-update) | async-done | bytes 1048592 | tf_op jit(solution)/shard_map/reduce_scatter | solution.py:129
  (189 shorter events, 23.9 us)
Async XLA Ops:
  6.5 451.0 %copy-start = (bf16[256,4096]{1,0:T(8,128)(2,1)S(1)}, bf16[256,4096]{1,0:T(8,128)(2,1)}, u32[]{:S(2)}) copy-start(bf16[256,4096]{1,0:T(8,128)(2,1)} %param.15) | copy-start | bytes 6291460
  6.5 116.0 %all-gather.3.cloned.1.call-start = ((), (), s32[]{:S(2)}) async-start(), calls=%async_computation.1 | async-start | bytes 9437184 | tf_op jit(solution)/shard_map/all_gather | solution.py:59
  10.7 119.7 %copy-start.3 = (bf16[4096,128]{1,0:T(8,128)(2,1)S(1)}, bf16[4096,128]{1,0:T(8,128)(2,1)}, u32[]{:S(2)}) copy-start(bf16[4096,128]{1,0:T(8,128)(2,1)} %param.14) | copy-start | bytes 3145732
  10.8 174.5 %all-gather.5.cloned.1.call-start = ((), (), s32[]{:S(2)}) async-start(), calls=%async_computation.2 | async-start | bytes 8912896 | tf_op jit(solution)/shard_map/all_gather | solution.py:114
  122.6 7.9 %copy-start.2 = (bf16[1,1024,4096]{2,1,0:T(8,128)(2,1)S(1)}, bf16[1,1024,4096]{2,1,0:T(8,128)(2,1)}, u32[]{:S(2)}) copy-start(bf16[1,1024,4096]{2,1,0:T(8,128)(2,1)} %all-gather.3.cloned.1.call-done) | copy-start | bytes 25165828
  130.5 8.1 %copy-start.5 = (s32[16]{0:T(128)S(1)}, s32[16]{0:T(128)}, u32[]{:S(2)}) copy-start(s32[16]{0:T(128)} %param.16) | copy-start | bytes 196
  134.2 444.5 %reduce-scatter.2.cloned.1.call-start = ((), (), s32[]{:S(2)}) async-start(), calls=%async_computation.3 | async-start | bytes 9437184 | tf_op jit(solution)/shard_map/reduce_scatter | solution.py:129
  139.9 45.4 %copy-start.4 = (s32[32]{0:T(128)S(1)}, s32[32]{0:T(128)}, u32[]{:S(2)}) copy-start(s32[32]{0:T(128)} %param.17) | copy-start | bytes 388
  193.0 7.0 %copy-start.1 = (f32[1024,1024,2]{1,0,2:T(8,128)S(1)}, f32[1024,1024,2]{1,0,2:T(8,128)}, u32[]{:S(2)}) copy-start(f32[1024,1024,2]{1,0,2:T(8,128)} %get-tuple-element.407) | copy-start | bytes 25165828 | tf_op jit(solution)/shard_map/while
  209.7 7.2 %copy-start.1 = (f32[1024,1024,2]{1,0,2:T(8,128)S(1)}, f32[1024,1024,2]{1,0,2:T(8,128)}, u32[]{:S(2)}) copy-start(f32[1024,1024,2]{1,0,2:T(8,128)} %get-tuple-element.407) | copy-start | bytes 25165828 | tf_op jit(solution)/shard_map/while
  226.7 7.2 %copy-start.1 = (f32[1024,1024,2]{1,0,2:T(8,128)S(1)}, f32[1024,1024,2]{1,0,2:T(8,128)}, u32[]{:S(2)}) copy-start(f32[1024,1024,2]{1,0,2:T(8,128)} %get-tuple-element.407) | copy-start | bytes 25165828 | tf_op jit(solution)/shard_map/while
  243.6 7.2 %copy-start.1 = (f32[1024,1024,2]{1,0,2:T(8,128)S(1)}, f32[1024,1024,2]{1,0,2:T(8,128)}, u32[]{:S(2)}) copy-start(f32[1024,1024,2]{1,0,2:T(8,128)} %get-tuple-element.407) | copy-start | bytes 25165828 | tf_op jit(solution)/shard_map/while
  260.6 7.2 %copy-start.1 = (f32[1024,1024,2]{1,0,2:T(8,128)S(1)}, f32[1024,1024,2]{1,0,2:T(8,128)}, u32[]{:S(2)}) copy-start(f32[1024,1024,2]{1,0,2:T(8,128)} %get-tuple-element.407) | copy-start | bytes 25165828 | tf_op jit(solution)/shard_map/while
  277.5 7.2 %copy-start.1 = (f32[1024,1024,2]{1,0,2:T(8,128)S(1)}, f32[1024,1024,2]{1,0,2:T(8,128)}, u32[]{:S(2)}) copy-start(f32[1024,1024,2]{1,0,2:T(8,128)} %get-tuple-element.407) | copy-start | bytes 25165828 | tf_op jit(solution)/shard_map/while
  294.5 7.2 %copy-start.1 = (f32[1024,1024,2]{1,0,2:T(8,128)S(1)}, f32[1024,1024,2]{1,0,2:T(8,128)}, u32[]{:S(2)}) copy-start(f32[1024,1024,2]{1,0,2:T(8,128)} %get-tuple-element.407) | copy-start | bytes 25165828 | tf_op jit(solution)/shard_map/while
  311.4 7.2 %copy-start.1 = (f32[1024,1024,2]{1,0,2:T(8,128)S(1)}, f32[1024,1024,2]{1,0,2:T(8,128)}, u32[]{:S(2)}) copy-start(f32[1024,1024,2]{1,0,2:T(8,128)} %get-tuple-element.407) | copy-start | bytes 25165828 | tf_op jit(solution)/shard_map/while
  328.4 7.2 %copy-start.1 = (f32[1024,1024,2]{1,0,2:T(8,128)S(1)}, f32[1024,1024,2]{1,0,2:T(8,128)}, u32[]{:S(2)}) copy-start(f32[1024,1024,2]{1,0,2:T(8,128)} %get-tuple-element.407) | copy-start | bytes 25165828 | tf_op jit(solution)/shard_map/while
  345.3 7.2 %copy-start.1 = (f32[1024,1024,2]{1,0,2:T(8,128)S(1)}, f32[1024,1024,2]{1,0,2:T(8,128)}, u32[]{:S(2)}) copy-start(f32[1024,1024,2]{1,0,2:T(8,128)} %get-tuple-element.407) | copy-start | bytes 25165828 | tf_op jit(solution)/shard_map/while
  362.3 7.2 %copy-start.1 = (f32[1024,1024,2]{1,0,2:T(8,128)S(1)}, f32[1024,1024,2]{1,0,2:T(8,128)}, u32[]{:S(2)}) copy-start(f32[1024,1024,2]{1,0,2:T(8,128)} %get-tuple-element.407) | copy-start | bytes 25165828 | tf_op jit(solution)/shard_map/while
  379.2 7.2 %copy-start.1 = (f32[1024,1024,2]{1,0,2:T(8,128)S(1)}, f32[1024,1024,2]{1,0,2:T(8,128)}, u32[]{:S(2)}) copy-start(f32[1024,1024,2]{1,0,2:T(8,128)} %get-tuple-element.407) | copy-start | bytes 25165828 | tf_op jit(solution)/shard_map/while
  396.2 7.2 %copy-start.1 = (f32[1024,1024,2]{1,0,2:T(8,128)S(1)}, f32[1024,1024,2]{1,0,2:T(8,128)}, u32[]{:S(2)}) copy-start(f32[1024,1024,2]{1,0,2:T(8,128)} %get-tuple-element.407) | copy-start | bytes 25165828 | tf_op jit(solution)/shard_map/while
  413.1 7.2 %copy-start.1 = (f32[1024,1024,2]{1,0,2:T(8,128)S(1)}, f32[1024,1024,2]{1,0,2:T(8,128)}, u32[]{:S(2)}) copy-start(f32[1024,1024,2]{1,0,2:T(8,128)} %get-tuple-element.407) | copy-start | bytes 25165828 | tf_op jit(solution)/shard_map/while
  430.1 7.2 %copy-start.1 = (f32[1024,1024,2]{1,0,2:T(8,128)S(1)}, f32[1024,1024,2]{1,0,2:T(8,128)}, u32[]{:S(2)}) copy-start(f32[1024,1024,2]{1,0,2:T(8,128)} %get-tuple-element.407) | copy-start | bytes 25165828 | tf_op jit(solution)/shard_map/while
  447.0 7.2 %copy-start.1 = (f32[1024,1024,2]{1,0,2:T(8,128)S(1)}, f32[1024,1024,2]{1,0,2:T(8,128)}, u32[]{:S(2)}) copy-start(f32[1024,1024,2]{1,0,2:T(8,128)} %get-tuple-element.407) | copy-start | bytes 25165828 | tf_op jit(solution)/shard_map/while
Sparse Core Ops, SparseCore 0:
  10.9 111.6 all-gather.2
  134.4 50.9 all-gather.4
  463.3 115.3 reduce-scatter.1
where the time goes:
time: 586 us; the launch traced here: 585 us
  waiting for transfers between devices  264 us (45%)
  matrix products  237 us (40%)
  other arithmetic  64.2 us (11%)
  between operations  13.3 us (2%)
    reduce_scatter x1, waiting for transfers between devices, per_device(): lax.psum_scatter(jnp.dot(attended, o_weight, preferred_element_type=jnp.f...  115 us
    dot_general x16, matrix products, attend(): jnp.einsum('kgqs,skd->qkgd', weights.astype(jnp.bfloat16), value_rows, pr...  115 us
    all_gather x1, waiting for transfers between devices, per_device(): portion = lax.all_gather(normed, 'tensor', axis=1, tiled=True)  111 us
    dot_general x16, matrix products, attend(): jnp.einsum('qkgd,skd->kgqs', queries, key_rows, preferred_element_type=jn...  100 us
    all_gather x1, waiting for transfers between devices, per_device(): gathered = lax.all_gather(kv_pair, 'context', axis=1, tiled=True)  37.5 us
    reduce_sum x16, other arithmetic, attend(): row_sum = row_sum * factor + jnp.sum(weights, axis=-1)  31.5 us
    and x16, other arithmetic, attend(): (key_places[None, :] <= query_places[:, None]) & (key_docs[None, :] == qu...  19.1 us
  transfers between devices with their start and end apart: 3, of which 3 were waited for; matrix products, arithmetic and copies ran while one was open for 2% of the time, Pallas kernels for 0%

commit v1 on v0

--- a/solution.py
+++ b/solution.py
@@ -111,7 +111,9 @@
         jnp.zeros((kv_local, group_size, tok_dev), jnp.float32),
         jnp.zeros((tok_dev, kv_local, group_size, head_dim), jnp.float32),
     )
-    gathered = lax.all_gather(kv_pair, "context", axis=1, tiled=True)
+    gathered = jnp.concatenate(
+        lax.all_to_all(jnp.stack([kv_pair] * lax.axis_size("context")), "context", 0, 0), axis=1
+    )
 
     def visit_block(block_index, carried):
         offset = block_index * tok_dev

time: 586 us -> 641 us (1.094)
  waiting for transfers between devices: 264 us -> 304 us
  local copies, waits for them, and re-layouts: 5.24 us -> 18.1 us
    all_to_all x0 -> x1, waiting for transfers between devices: none -> 81.5 us  [per_device(): lax.all_to_all(jnp.stack([kv_pair] * lax.axis_size('context')), 'context'...]
    all_gather x1 -> x0, waiting for transfers between devices: 37.5 us -> none  [per_device(): gathered = lax.all_gather(kv_pair, 'context', axis=1, tiled=True)]
    all_to_all x0 -> x1, local copies, waits for them, and re-layouts: none -> 7.51 us  [per_device(): lax.all_to_all(jnp.stack([kv_pair] * lax.axis_size('context')), 'context'...]
where the time goes in v1:
time: 641 us; the launch traced here: 640 us
  waiting for transfers between devices  304 us (47%)
  matrix products  233 us (36%)
  other arithmetic  63.5 us (10%)
  local copies, waits for them, and re-layouts  18.1 us (3%)
  between operations  13.6 us (2%)
    dot_general x16, matrix products, attend(): jnp.einsum('kgqs,skd->qkgd', weights.astype(jnp.bfloat16), value_rows, pr...  114 us
    reduce_scatter x1, waiting for transfers between devices, per_device(): lax.psum_scatter(jnp.dot(attended, o_weight, preferred_element_type=jnp.f...  112 us
    all_gather x1, waiting for transfers between devices, per_device(): portion = lax.all_gather(normed, 'tensor', axis=1, tiled=True)  111 us
    dot_general x16, matrix products, attend(): jnp.einsum('qkgd,skd->kgqs', queries, key_rows, preferred_element_type=jn...  98 us
    all_to_all x1, waiting for transfers between devices, per_device(): lax.all_to_all(jnp.stack([kv_pair] * lax.axis_size('context')), 'context'...  81.5 us
    reduce_sum x16, other arithmetic, attend(): row_sum = row_sum * factor + jnp.sum(weights, axis=-1)  31.5 us
    and x16, other arithmetic, attend(): (key_places[None, :] <= query_places[:, None]) & (key_docs[None, :] == qu...  19.1 us
  transfers between devices with their start and end apart: 3, of which 3 were waited for; matrix products, arithmetic and copies ran while one was open for 2% of the time, Pallas kernels for 0%

profile of v1, /device:TPU:1, one launch (start us, length us, event | category | flops | bytes accessed | tf_op | source)
XLA Modules:
  0.0 640.0 jit_solution(6209834441240537270)
XLA Ops:
  6.5 1.7 fusion.34
  8.2 2.5 fusion.36
  11.7 110.9 %all-gather.2.cloned.1.call-done = bf16[1,1024,4096]{2,1,0:T(8,128)(2,1)} async-done(((bf16[1,128,4096]{2,1,0:T(8,128)(2,1)}), bf16[1,1024,4096]{2,1,0:T(8,128)(2,1)}) %all-gather.2.cloned.1.call-update) | async-done | bytes 8388624 | tf_op jit(solution)/shard_map/all_gather | solution.py:59
  122.6 6.7 %fusion.37 = f32[1024,1,128]{0,2,1:T(8,128)S(1)} fusion(bf16[4096,128]{1,0:T(8,128)(2,1)} %param.13, bf16[1,1024,4096]{2,1,0:T(8,128)(2,1)} %all-gather.2.cloned.1.call-done), kind=kOutput, calls=%fused_computation.56 | convolution fusion | flops 1073741824 | bytes 9961472 | tf_op jit(solution)/shard_map/dot_general | solution.py:66
  130.5 2.9 fusion.43
  133.7 5.1 stack.8
  138.8 5.7 all-to-all-start
  144.8 4.1 copy.38
  150.2 6.3 fusion.28
  157.8 81.5 %all-to-all-done = bf16[16,2,1024,128]{3,2,1,0:T(8,128)(2,1)} async-done(((bf16[16,2,1024,128]{3,2,1,0:T(8,128)(2,1)}), bf16[16,2,1024,128]{3,2,1,0:T(8,128)(2,1)}, u32[]{:S(2)}, u32[]{:S(2)}) %all-to-all-start) | async-done | bytes 8388640 | tf_op jit(solution)/shard_map/all_to_all | solution.py:115
  239.3 7.5 %copy.32 = bf16[16,2,1024,128]{3,2,0,1:T(8,128)(2,1)} copy(bf16[16,2,1024,128]{3,2,1,0:T(8,128)(2,1)} %all-to-all-done) | data formatting | bytes 16777216 | tf_op jit(solution)/shard_map/all_to_all | solution.py:115
  246.8 267.6 %while.20 = (s32[]{:T(128)}, f32[1,2,1024]{2,1,0:T(2,128)S(1)}, f32[1,2,1024]{2,1,0:T(2,128)S(1)}, f32[1024,1,2,128]{0,3,2,1:T(8,128)}, s32[32]{0:T(128)S(1)}, /...) while((s32[]{:T(128)}, f32[1,2,1024]{2,1,0:T(2,128)S(1)}, ...), condition=%wide.region_9.10_spmd.clone, body=%wide.region_4.9_spmd.clone.sunk | while | flops 1100931072 | bytes 66236864 | solution.py:123
  247.0 1.2 compare_and_fusion.2
  248.2 6.1 fusion.77
  254.4 6.9 %fusion.80 = f32[1024,1,2,128]{0,3,2,1:T(8,128)} fusion(f32[1024,1024,2]{1,0,2:T(8,128)} %get-tuple-element.427, f32[2,1024]{1,0:T(2,128)S(1)} %bitcast.128, pred[1024,1024]{0,1:T(8,128)(4,1)S(1)} %compare_and_fusion.2, f32[1024,1,2,128]{0,3,2,1:T(8,128)} %get-tuple-element.447, f32[1024,2]{0,1:T(2,128)S(1)} %get-tuple-element.428, ...), kind=kOutput, calls=%fused_computation.12.clone.1 | convolution fusion | flops 546045952 | bytes 11812873 | tf_op jit(solution)/shard_map/while/body/eval_jaxpr/kgqs,skd->qkgd/dot_general | solution.py:101
  261.3 2.0 fusion.79
  264.7 6.1 fusion.77
  270.9 7.1 %fusion.80 = f32[1024,1,2,128]{0,3,2,1:T(8,128)} fusion(f32[1024,1024,2]{1,0,2:T(8,128)} %get-tuple-element.427, f32[2,1024]{1,0:T(2,128)S(1)} %bitcast.128, pred[1024,1024]{0,1:T(8,128)(4,1)S(1)} %compare_and_fusion.2, f32[1024,1,2,128]{0,3,2,1:T(8,128)} %get-tuple-element.447, f32[1024,2]{0,1:T(2,128)S(1)} %get-tuple-element.428, ...), kind=kOutput, calls=%fused_computation.12.clone.1 | convolution fusion | flops 546045952 | bytes 11812873 | tf_op jit(solution)/shard_map/while/body/eval_jaxpr/kgqs,skd->qkgd/dot_general | solution.py:101
  278.0 2.0 fusion.79
  281.5 6.1 fusion.77
  287.6 7.1 %fusion.80 = f32[1024,1,2,128]{0,3,2,1:T(8,128)} fusion(f32[1024,1024,2]{1,0,2:T(8,128)} %get-tuple-element.427, f32[2,1024]{1,0:T(2,128)S(1)} %bitcast.128, pred[1024,1024]{0,1:T(8,128)(4,1)S(1)} %compare_and_fusion.2, f32[1024,1,2,128]{0,3,2,1:T(8,128)} %get-tuple-element.447, f32[1024,2]{0,1:T(2,128)S(1)} %get-tuple-element.428, ...), kind=kOutput, calls=%fused_computation.12.clone.1 | convolution fusion | flops 546045952 | bytes 11812873 | tf_op jit(solution)/shard_map/while/body/eval_jaxpr/kgqs,skd->qkgd/dot_general | solution.py:101
  294.7 2.0 fusion.79
  298.2 6.1 fusion.77
  304.4 7.1 %fusion.80 = f32[1024,1,2,128]{0,3,2,1:T(8,128)} fusion(f32[1024,1024,2]{1,0,2:T(8,128)} %get-tuple-element.427, f32[2,1024]{1,0:T(2,128)S(1)} %bitcast.128, pred[1024,1024]{0,1:T(8,128)(4,1)S(1)} %compare_and_fusion.2, f32[1024,1,2,128]{0,3,2,1:T(8,128)} %get-tuple-element.447, f32[1024,2]{0,1:T(2,128)S(1)} %get-tuple-element.428, ...), kind=kOutput, calls=%fused_computation.12.clone.1 | convolution fusion | flops 546045952 | bytes 11812873 | tf_op jit(solution)/shard_map/while/body/eval_jaxpr/kgqs,skd->qkgd/dot_general | solution.py:101
  311.5 2.0 fusion.79
  314.9 6.1 fusion.77
  321.1 7.1 %fusion.80 = f32[1024,1,2,128]{0,3,2,1:T(8,128)} fusion(f32[1024,1024,2]{1,0,2:T(8,128)} %get-tuple-element.427, f32[2,1024]{1,0:T(2,128)S(1)} %bitcast.128, pred[1024,1024]{0,1:T(8,128)(4,1)S(1)} %compare_and_fusion.2, f32[1024,1,2,128]{0,3,2,1:T(8,128)} %get-tuple-element.447, f32[1024,2]{0,1:T(2,128)S(1)} %get-tuple-element.428, ...), kind=kOutput, calls=%fused_computation.12.clone.1 | convolution fusion | flops 546045952 | bytes 11812873 | tf_op jit(solution)/shard_map/while/body/eval_jaxpr/kgqs,skd->qkgd/dot_general | solution.py:101
  328.2 2.0 fusion.79
  331.7 6.1 fusion.77
  337.8 7.1 %fusion.80 = f32[1024,1,2,128]{0,3,2,1:T(8,128)} fusion(f32[1024,1024,2]{1,0,2:T(8,128)} %get-tuple-element.427, f32[2,1024]{1,0:T(2,128)S(1)} %bitcast.128, pred[1024,1024]{0,1:T(8,128)(4,1)S(1)} %compare_and_fusion.2, f32[1024,1,2,128]{0,3,2,1:T(8,128)} %get-tuple-element.447, f32[1024,2]{0,1:T(2,128)S(1)} %get-tuple-element.428, ...), kind=kOutput, calls=%fused_computation.12.clone.1 | convolution fusion | flops 546045952 | bytes 11812873 | tf_op jit(solution)/shard_map/while/body/eval_jaxpr/kgqs,skd->qkgd/dot_general | solution.py:101
  345.0 2.0 fusion.79
  348.4 6.1 fusion.77
  354.6 7.1 %fusion.80 = f32[1024,1,2,128]{0,3,2,1:T(8,128)} fusion(f32[1024,1024,2]{1,0,2:T(8,128)} %get-tuple-element.427, f32[2,1024]{1,0:T(2,128)S(1)} %bitcast.128, pred[1024,1024]{0,1:T(8,128)(4,1)S(1)} %compare_and_fusion.2, f32[1024,1,2,128]{0,3,2,1:T(8,128)} %get-tuple-element.447, f32[1024,2]{0,1:T(2,128)S(1)} %get-tuple-element.428, ...), kind=kOutput, calls=%fused_computation.12.clone.1 | convolution fusion | flops 546045952 | bytes 11812873 | tf_op jit(solution)/shard_map/while/body/eval_jaxpr/kgqs,skd->qkgd/dot_general | solution.py:101
  361.7 2.0 fusion.79
  365.2 6.1 fusion.77
  371.3 7.1 %fusion.80 = f32[1024,1,2,128]{0,3,2,1:T(8,128)} fusion(f32[1024,1024,2]{1,0,2:T(8,128)} %get-tuple-element.427, f32[2,1024]{1,0:T(2,128)S(1)} %bitcast.128, pred[1024,1024]{0,1:T(8,128)(4,1)S(1)} %compare_and_fusion.2, f32[1024,1,2,128]{0,3,2,1:T(8,128)} %get-tuple-element.447, f32[1024,2]{0,1:T(2,128)S(1)} %get-tuple-element.428, ...), kind=kOutput, calls=%fused_computation.12.clone.1 | convolution fusion | flops 546045952 | bytes 11812873 | tf_op jit(solution)/shard_map/while/body/eval_jaxpr/kgqs,skd->qkgd/dot_general | solution.py:101
  378.5 2.0 fusion.79
  381.9 6.1 fusion.77
  388.1 7.1 %fusion.80 = f32[1024,1,2,128]{0,3,2,1:T(8,128)} fusion(f32[1024,1024,2]{1,0,2:T(8,128)} %get-tuple-element.427, f32[2,1024]{1,0:T(2,128)S(1)} %bitcast.128, pred[1024,1024]{0,1:T(8,128)(4,1)S(1)} %compare_and_fusion.2, f32[1024,1,2,128]{0,3,2,1:T(8,128)} %get-tuple-element.447, f32[1024,2]{0,1:T(2,128)S(1)} %get-tuple-element.428, ...), kind=kOutput, calls=%fused_computation.12.clone.1 | convolution fusion | flops 546045952 | bytes 11812873 | tf_op jit(solution)/shard_map/while/body/eval_jaxpr/kgqs,skd->qkgd/dot_general | solution.py:101
  395.2 2.0 fusion.79
  398.6 6.1 fusion.77
  404.8 7.1 %fusion.80 = f32[1024,1,2,128]{0,3,2,1:T(8,128)} fusion(f32[1024,1024,2]{1,0,2:T(8,128)} %get-tuple-element.427, f32[2,1024]{1,0:T(2,128)S(1)} %bitcast.128, pred[1024,1024]{0,1:T(8,128)(4,1)S(1)} %compare_and_fusion.2, f32[1024,1,2,128]{0,3,2,1:T(8,128)} %get-tuple-element.447, f32[1024,2]{0,1:T(2,128)S(1)} %get-tuple-element.428, ...), kind=kOutput, calls=%fused_computation.12.clone.1 | convolution fusion | flops 546045952 | bytes 11812873 | tf_op jit(solution)/shard_map/while/body/eval_jaxpr/kgqs,skd->qkgd/dot_general | solution.py:101
  411.9 2.0 fusion.79
  415.4 6.1 fusion.77
  421.5 7.1 %fusion.80 = f32[1024,1,2,128]{0,3,2,1:T(8,128)} fusion(f32[1024,1024,2]{1,0,2:T(8,128)} %get-tuple-element.427, f32[2,1024]{1,0:T(2,128)S(1)} %bitcast.128, pred[1024,1024]{0,1:T(8,128)(4,1)S(1)} %compare_and_fusion.2, f32[1024,1,2,128]{0,3,2,1:T(8,128)} %get-tuple-element.447, f32[1024,2]{0,1:T(2,128)S(1)} %get-tuple-element.428, ...), kind=kOutput, calls=%fused_computation.12.clone.1 | convolution fusion | flops 546045952 | bytes 11812873 | tf_op jit(solution)/shard_map/while/body/eval_jaxpr/kgqs,skd->qkgd/dot_general | solution.py:101
  428.7 2.0 fusion.79
  432.1 6.1 fusion.77
  438.3 7.1 %fusion.80 = f32[1024,1,2,128]{0,3,2,1:T(8,128)} fusion(f32[1024,1024,2]{1,0,2:T(8,128)} %get-tuple-element.427, f32[2,1024]{1,0:T(2,128)S(1)} %bitcast.128, pred[1024,1024]{0,1:T(8,128)(4,1)S(1)} %compare_and_fusion.2, f32[1024,1,2,128]{0,3,2,1:T(8,128)} %get-tuple-element.447, f32[1024,2]{0,1:T(2,128)S(1)} %get-tuple-element.428, ...), kind=kOutput, calls=%fused_computation.12.clone.1 | convolution fusion | flops 546045952 | bytes 11812873 | tf_op jit(solution)/shard_map/while/body/eval_jaxpr/kgqs,skd->qkgd/dot_general | solution.py:101
  445.4 2.0 fusion.79
  448.9 6.1 fusion.77
  455.0 7.1 %fusion.80 = f32[1024,1,2,128]{0,3,2,1:T(8,128)} fusion(f32[1024,1024,2]{1,0,2:T(8,128)} %get-tuple-element.427, f32[2,1024]{1,0:T(2,128)S(1)} %bitcast.128, pred[1024,1024]{0,1:T(8,128)(4,1)S(1)} %compare_and_fusion.2, f32[1024,1,2,128]{0,3,2,1:T(8,128)} %get-tuple-element.447, f32[1024,2]{0,1:T(2,128)S(1)} %get-tuple-element.428, ...), kind=kOutput, calls=%fused_computation.12.clone.1 | convolution fusion | flops 546045952 | bytes 11812873 | tf_op jit(solution)/shard_map/while/body/eval_jaxpr/kgqs,skd->qkgd/dot_general | solution.py:101
  462.2 2.0 fusion.79
  465.6 6.1 fusion.77
  471.8 7.1 %fusion.80 = f32[1024,1,2,128]{0,3,2,1:T(8,128)} fusion(f32[1024,1024,2]{1,0,2:T(8,128)} %get-tuple-element.427, f32[2,1024]{1,0:T(2,128)S(1)} %bitcast.128, pred[1024,1024]{0,1:T(8,128)(4,1)S(1)} %compare_and_fusion.2, f32[1024,1,2,128]{0,3,2,1:T(8,128)} %get-tuple-element.447, f32[1024,2]{0,1:T(2,128)S(1)} %get-tuple-element.428, ...), kind=kOutput, calls=%fused_computation.12.clone.1 | convolution fusion | flops 546045952 | bytes 11812873 | tf_op jit(solution)/shard_map/while/body/eval_jaxpr/kgqs,skd->qkgd/dot_general | solution.py:101
  478.9 2.0 fusion.79
  482.4 6.1 fusion.77
  488.5 7.1 %fusion.80 = f32[1024,1,2,128]{0,3,2,1:T(8,128)} fusion(f32[1024,1024,2]{1,0,2:T(8,128)} %get-tuple-element.427, f32[2,1024]{1,0:T(2,128)S(1)} %bitcast.128, pred[1024,1024]{0,1:T(8,128)(4,1)S(1)} %compare_and_fusion.2, f32[1024,1,2,128]{0,3,2,1:T(8,128)} %get-tuple-element.447, f32[1024,2]{0,1:T(2,128)S(1)} %get-tuple-element.428, ...), kind=kOutput, calls=%fused_computation.12.clone.1 | convolution fusion | flops 546045952 | bytes 11812873 | tf_op jit(solution)/shard_map/while/body/eval_jaxpr/kgqs,skd->qkgd/dot_general | solution.py:101
  495.6 2.0 fusion.79
  499.1 6.1 fusion.77
  505.2 7.1 %fusion.80 = f32[1024,1,2,128]{0,3,2,1:T(8,128)} fusion(f32[1024,1024,2]{1,0,2:T(8,128)} %get-tuple-element.427, f32[2,1024]{1,0:T(2,128)S(1)} %bitcast.128, pred[1024,1024]{0,1:T(8,128)(4,1)S(1)} %compare_and_fusion.2, f32[1024,1,2,128]{0,3,2,1:T(8,128)} %get-tuple-element.447, f32[1024,2]{0,1:T(2,128)S(1)} %get-tuple-element.428, ...), kind=kOutput, calls=%fused_computation.12.clone.1 | convolution fusion | flops 546045952 | bytes 11812873 | tf_op jit(solution)/shard_map/while/body/eval_jaxpr/kgqs,skd->qkgd/dot_general | solution.py:101
  512.4 2.0 fusion.79
  514.4 1.3 divide_convert_fusion
  515.7 5.6 convolution_convert_fusion
  521.4 111.8 %reduce-scatter.2.cloned.1.call-done = bf16[128,4096]{1,0:T(8,128)(2,1)} async-done(((bf16[1024,4096]{1,0:T(8,128)(2,1)}), bf16[128,4096]{1,0:T(8,128)(2,1)}) %reduce-scatter.2.cloned.1.call-update) | async-done | bytes 1048592 | tf_op jit(solution)/shard_map/reduce_scatter | solution.py:131
  (191 shorter events, 27.0 us)
Async XLA Ops:
  6.5 509.2 %copy-start = (bf16[256,4096]{1,0:T(8,128)(2,1)S(1)}, bf16[256,4096]{1,0:T(8,128)(2,1)}, u32[]{:S(2)}) copy-start(bf16[256,4096]{1,0:T(8,128)(2,1)} %param.15) | copy-start | bytes 6291460
  6.5 116.0 %all-gather.2.cloned.1.call-start = ((), (), s32[]{:S(2)}) async-start(), calls=%async_computation.2 | async-start | bytes 9437184 | tf_op jit(solution)/shard_map/all_gather | solution.py:59
  10.7 119.7 %copy-start.3 = (bf16[4096,128]{1,0:T(8,128)(2,1)S(1)}, bf16[4096,128]{1,0:T(8,128)(2,1)}, u32[]{:S(2)}) copy-start(bf16[4096,128]{1,0:T(8,128)(2,1)} %param.14) | copy-start | bytes 3145732
  122.6 7.9 %copy-start.2 = (bf16[1,1024,4096]{2,1,0:T(8,128)(2,1)S(1)}, bf16[1,1024,4096]{2,1,0:T(8,128)(2,1)}, u32[]{:S(2)}) copy-start(bf16[1,1024,4096]{2,1,0:T(8,128)(2,1)} %all-gather.2.cloned.1.call-done) | copy-start | bytes 25165828
  138.8 10.1 %copy-start.5 = (s32[16]{0:T(128)S(1)}, s32[16]{0:T(128)}, u32[]{:S(2)}) copy-start(s32[16]{0:T(128)} %param.16) | copy-start | bytes 196
  138.8 100.4 %all-to-all-start = ((bf16[16,2,1024,128]{3,2,1,0:T(8,128)(2,1)}), bf16[16,2,1024,128]{3,2,1,0:T(8,128)(2,1)}, u32[]{:S(2)}, u32[]{:S(2)}) async-start(bf16[16,2,1024,128]{3,2,1,0:T(8,128)(2,1)} %stack.8), calls=%async_computation | async-start | bytes 16777216 | tf_op jit(solution)/shard_map/all_to_all | solution.py:115
  144.6 488.6 %reduce-scatter.2.cloned.1.call-start = ((), (), s32[]{:S(2)}) async-start(), calls=%async_computation.3 | async-start | bytes 9437184 | tf_op jit(solution)/shard_map/reduce_scatter | solution.py:131
  157.8 89.0 %copy-start.4 = (s32[32]{0:T(128)S(1)}, s32[32]{0:T(128)}, u32[]{:S(2)}) copy-start(s32[32]{0:T(128)} %param.17) | copy-start | bytes 388
  254.3 6.9 %copy-start.1 = (f32[1024,1024,2]{1,0,2:T(8,128)S(1)}, f32[1024,1024,2]{1,0,2:T(8,128)}, u32[]{:S(2)}) copy-start(f32[1024,1024,2]{1,0,2:T(8,128)} %get-tuple-element.427) | copy-start | bytes 25165828 | tf_op jit(solution)/shard_map/while
  270.9 7.1 %copy-start.1 = (f32[1024,1024,2]{1,0,2:T(8,128)S(1)}, f32[1024,1024,2]{1,0,2:T(8,128)}, u32[]{:S(2)}) copy-start(f32[1024,1024,2]{1,0,2:T(8,128)} %get-tuple-element.427) | copy-start | bytes 25165828 | tf_op jit(solution)/shard_map/while
  287.6 7.1 %copy-start.1 = (f32[1024,1024,2]{1,0,2:T(8,128)S(1)}, f32[1024,1024,2]{1,0,2:T(8,128)}, u32[]{:S(2)}) copy-start(f32[1024,1024,2]{1,0,2:T(8,128)} %get-tuple-element.427) | copy-start | bytes 25165828 | tf_op jit(solution)/shard_map/while
  304.3 7.1 %copy-start.1 = (f32[1024,1024,2]{1,0,2:T(8,128)S(1)}, f32[1024,1024,2]{1,0,2:T(8,128)}, u32[]{:S(2)}) copy-start(f32[1024,1024,2]{1,0,2:T(8,128)} %get-tuple-element.427) | copy-start | bytes 25165828 | tf_op jit(solution)/shard_map/while
  321.1 7.1 %copy-start.1 = (f32[1024,1024,2]{1,0,2:T(8,128)S(1)}, f32[1024,1024,2]{1,0,2:T(8,128)}, u32[]{:S(2)}) copy-start(f32[1024,1024,2]{1,0,2:T(8,128)} %get-tuple-element.427) | copy-start | bytes 25165828 | tf_op jit(solution)/shard_map/while
  337.8 7.1 %copy-start.1 = (f32[1024,1024,2]{1,0,2:T(8,128)S(1)}, f32[1024,1024,2]{1,0,2:T(8,128)}, u32[]{:S(2)}) copy-start(f32[1024,1024,2]{1,0,2:T(8,128)} %get-tuple-element.427) | copy-start | bytes 25165828 | tf_op jit(solution)/shard_map/while
  354.6 7.1 %copy-start.1 = (f32[1024,1024,2]{1,0,2:T(8,128)S(1)}, f32[1024,1024,2]{1,0,2:T(8,128)}, u32[]{:S(2)}) copy-start(f32[1024,1024,2]{1,0,2:T(8,128)} %get-tuple-element.427) | copy-start | bytes 25165828 | tf_op jit(solution)/shard_map/while
  371.3 7.1 %copy-start.1 = (f32[1024,1024,2]{1,0,2:T(8,128)S(1)}, f32[1024,1024,2]{1,0,2:T(8,128)}, u32[]{:S(2)}) copy-start(f32[1024,1024,2]{1,0,2:T(8,128)} %get-tuple-element.427) | copy-start | bytes 25165828 | tf_op jit(solution)/shard_map/while
  388.0 7.1 %copy-start.1 = (f32[1024,1024,2]{1,0,2:T(8,128)S(1)}, f32[1024,1024,2]{1,0,2:T(8,128)}, u32[]{:S(2)}) copy-start(f32[1024,1024,2]{1,0,2:T(8,128)} %get-tuple-element.427) | copy-start | bytes 25165828 | tf_op jit(solution)/shard_map/while
  404.8 7.1 %copy-start.1 = (f32[1024,1024,2]{1,0,2:T(8,128)S(1)}, f32[1024,1024,2]{1,0,2:T(8,128)}, u32[]{:S(2)}) copy-start(f32[1024,1024,2]{1,0,2:T(8,128)} %get-tuple-element.427) | copy-start | bytes 25165828 | tf_op jit(solution)/shard_map/while
  421.5 7.1 %copy-start.1 = (f32[1024,1024,2]{1,0,2:T(8,128)S(1)}, f32[1024,1024,2]{1,0,2:T(8,128)}, u32[]{:S(2)}) copy-start(f32[1024,1024,2]{1,0,2:T(8,128)} %get-tuple-element.427) | copy-start | bytes 25165828 | tf_op jit(solution)/shard_map/while
  438.3 7.1 %copy-start.1 = (f32[1024,1024,2]{1,0,2:T(8,128)S(1)}, f32[1024,1024,2]{1,0,2:T(8,128)}, u32[]{:S(2)}) copy-start(f32[1024,1024,2]{1,0,2:T(8,128)} %get-tuple-element.427) | copy-start | bytes 25165828 | tf_op jit(solution)/shard_map/while
  455.0 7.1 %copy-start.1 = (f32[1024,1024,2]{1,0,2:T(8,128)S(1)}, f32[1024,1024,2]{1,0,2:T(8,128)}, u32[]{:S(2)}) copy-start(f32[1024,1024,2]{1,0,2:T(8,128)} %get-tuple-element.427) | copy-start | bytes 25165828 | tf_op jit(solution)/shard_map/while
  471.8 7.1 %copy-start.1 = (f32[1024,1024,2]{1,0,2:T(8,128)S(1)}, f32[1024,1024,2]{1,0,2:T(8,128)}, u32[]{:S(2)}) copy-start(f32[1024,1024,2]{1,0,2:T(8,128)} %get-tuple-element.427) | copy-start | bytes 25165828 | tf_op jit(solution)/shard_map/while
  488.5 7.1 %copy-start.1 = (f32[1024,1024,2]{1,0,2:T(8,128)S(1)}, f32[1024,1024,2]{1,0,2:T(8,128)}, u32[]{:S(2)}) copy-start(f32[1024,1024,2]{1,0,2:T(8,128)} %get-tuple-element.427) | copy-start | bytes 25165828 | tf_op jit(solution)/shard_map/while
  505.2 7.1 %copy-start.1 = (f32[1024,1024,2]{1,0,2:T(8,128)S(1)}, f32[1024,1024,2]{1,0,2:T(8,128)}, u32[]{:S(2)}) copy-start(f32[1024,1024,2]{1,0,2:T(8,128)} %get-tuple-element.427) | copy-start | bytes 25165828 | tf_op jit(solution)/shard_map/while
Sparse Core Ops, SparseCore 0:
  10.9 111.6 all-gather.1
  521.5 111.6 reduce-scatter.1
